TPU v7x, 32 devices: a whole 2x2x4 slice. The times are simulated.
32 devices in a mesh: inter: 16 (over z, y, x), intra: 2 (over core).
Axes of the slice: x: 2, y: 2, z: 4, core: 2. Of those that a mesh axis runs over, the one named last changes fastest.
Arguments:
- tokens: bfloat16 [2048, 4096], P('inter', 'intra'), may hold values from -6 to 6
- gate_codes: bfloat16 [7168, 4096], P(('intra', 'inter')), may hold values from -127 to 127
- gate_scales: float32 [7168, 16], P(('intra', 'inter')), may hold values from 0.0001 to 0.0005
- up_codes: bfloat16 [7168, 4096], P(('intra', 'inter')), may hold values from -127 to 127
- up_scales: float32 [7168, 16], P(('intra', 'inter')), may hold values from 0.0001 to 0.0005
- cotangent: bfloat16 [2048, 7168], P('inter', 'intra'), may hold values from -6 to 6
Outputs:
- hidden: bfloat16 [2048, 7168], P('inter', 'intra')
- token_grad: bfloat16 [2048, 4096], P('inter', 'intra')
- gate_grad: float32 [7168, 4096], P(('intra', 'inter'))
- up_grad: float32 [7168, 4096], P(('intra', 'inter'))
All inputs are finite; a program needn't handle non-finite values.
Results may differ from a plain program's by a relative error of at most 0.02.
Values may be sent and summed in bfloat16 or wider, within the bound.
A program may use at most 384 MiB of HBM per device.

v0:
```python
import jax
import jax.numpy as jnp
from jax import lax
from jax.sharding import PartitionSpec as P


def dequantize(codes, scales):
    rows, width = codes.shape
    blocks = scales.shape[1]
    step = width // blocks
    parts = [
        codes[:, b * step : (b + 1) * step].astype(jnp.float32) * scales[:, b : b + 1]
        for b in range(blocks)
    ]
    return jnp.concatenate(parts, axis=1).astype(jnp.bfloat16)


def per_device(tokens, gate_codes, gate_scales, up_codes, up_scales, cotangent):
    groups = lax.axis_size("inter")
    mine = lax.all_gather(tokens, "inter", axis=0, tiled=True)
    whole = lax.all_gather(mine, "intra", axis=0, tiled=False)
    slabs, count, wide = whole.shape
    back = lax.all_to_all(cotangent, "inter", split_axis=1, concat_axis=0, tiled=True)
    w_gate = dequantize(gate_codes, gate_scales)
    w_up = dequantize(up_codes, up_scales)

    def forward(weights):
        total = None
        for s in range(slabs):
            term = lax.dot_general(
                whole[s],
                weights[:, s * wide : (s + 1) * wide],
                (((1,), (1,)), ((), ())),
                preferred_element_type=jnp.float32,
            )
            total = term if total is None else total + term
        return total

    gate = forward(w_gate)
    up = forward(w_up)
    sig = jax.nn.sigmoid(gate)
    act = gate * sig
    hidden = (act * up).astype(jnp.bfloat16)
    back = back.astype(jnp.float32)
    d_up = (back * act).astype(jnp.bfloat16)
    d_gate = (back * up * sig * (1.0 + gate * (1.0 - sig))).astype(jnp.bfloat16)
    hidden = lax.all_to_all(hidden, "inter", split_axis=0, concat_axis=1, tiled=True)
    partial_sum = jnp.dot(d_gate, w_gate, preferred_element_type=jnp.float32)
    partial_sum = partial_sum + jnp.dot(d_up, w_up, preferred_element_type=jnp.float32)
    partial_sum = lax.psum_scatter(
        partial_sum.astype(jnp.bfloat16), "intra", scatter_dimension=1, tiled=True
    )
    token_grad = lax.psum_scatter(partial_sum, "inter", scatter_dimension=0, tiled=True)

    def rows_grad(d_rows):
        terms = [
            lax.dot_general(
                d_rows, whole[s], (((0,), (0,)), ((), ())), preferred_element_type=jnp.float32
            )
            for s in range(slabs)
        ]
        return jnp.concatenate(terms, axis=1) / groups

    return (hidden, token_grad, rows_grad(d_gate), rows_grad(d_up))


def solution(mesh):
    return jax.shard_map(
        per_device,
        mesh=mesh,
        in_specs=(
            P("inter", "intra"),
            P(("intra", "inter"), None),
            P(("intra", "inter"), None),
            P(("intra", "inter"), None),
            P(("intra", "inter"), None),
            P("inter", "intra"),
        ),
        out_specs=(
            P("inter", "intra"),
            P("inter", "intra"),
            P(("intra", "inter"), None),
            P(("intra", "inter"), None),
        ),
        check_vma=False,
    )
```

profile of v0, /device:TPU:26, one launch (start us, length us, event | category | flops | bytes accessed | tf_op | source)
XLA Modules:
  0.0 465.3 jit_solution(1570176110932852104)
XLA Ops:
  7.9 114.0 %all-gather.4.cloned.1.call-done = bf16[2048,2048]{1,0:T(8,128)(2,1)} async-done(((bf16[128,2048]{1,0:T(8,128)(2,1)}), bf16[2048,2048]{1,0:T(8,128)(2,1)}) %all-gather.4.cloned.1.call-update) | async-done | bytes 8388624 | tf_op jit(solution)/shard_map/all_gather | solution.py:20
  124.4 6.3 %all-to-all-start.1 = ((bf16[128,16,224]{0,2,1:T(8,128)(2,1)}), bf16[128,16,224]{0,2,1:T(8,128)(2,1)S(1)}, u32[]{:S(2)}, u32[]{:S(2)}) async-start(bf16[128,16,224]{0,2,1:T(8,128)(2,1)} %bitcast.36), calls=%async_computation.1 | async-start | bytes 1835008 | tf_op jit(solution)/shard_map/all_to_all | solution.py:23
  141.2 1.7 constant_dynamic-update-slice_fusion.47
  143.0 1.7 constant_dynamic-update-slice_fusion.46
  144.7 1.7 constant_dynamic-update-slice_fusion.45
  154.6 1.8 constant_dynamic-update-slice_fusion.39
  164.3 1.7 constant_dynamic-update-slice_fusion.38
  166.0 1.7 constant_dynamic-update-slice_fusion.37
  169.4 1.7 constant_dynamic-update-slice_fusion.35
  176.1 7.7 %fusion.2 = f32[224,2048]{1,0:T(8,128)} fusion(bf16[224,2048]{1,0:T(8,128)(2,1)} %copy-done.7, bf16[4096,2048]{1,0:T(8,128)(2,1)} %all-gather.6.cloned.1.call-done), kind=kOutput, calls=%fused_computation.3 | convolution fusion | flops 1879048192 | bytes 11141120 | tf_op jit(solution)/shard_map/dot_general | solution.py:30
  183.8 6.7 %fusion.4 = f32[224,2048]{1,0:T(8,128)S(1)} fusion(bf16[224,2048]{1,0:T(8,128)(2,1)} %get-tuple-element.44, bf16[4096,2048]{1,0:T(8,128)(2,1)} %all-gather.6.cloned.1.call-done), kind=kOutput, calls=%fused_computation.5 | convolution fusion | flops 1879048192 | bytes 11141120 | tf_op jit(solution)/shard_map/dot_general | solution.py:30
  190.5 3.9 fusion.19
  195.3 9.3 %fusion.31 = (bf16[2048,224]{0,1:T(8,128)(2,1)S(1)}, bf16[2048,224]{0,1:T(8,128)(2,1)S(1)}, bf16[28,16,8,128]{3,2,1,0:T(8,128)(2,1)}) fusion(f32[2048,224]{0,1:T(8,128)} %fusion.19, f32[224,2048]{1,0:T(8,128)} %fusion.2, bf16[224,2048]{1,0:T(8,128)(2,1)} %copy-done.8, bf16[4096,2048]{1,0:T(8,128)(2,1)} %all-gather.6.cloned.1.call-done, ...), kind=kOutput, calls=%fused_computation.28 | convolution fusion | flops 1886846976 | bytes 16646144 | tf_op jit(solution)/shard_map/dot_general | solution.py:30
  204.6 15.0 %fusion.38 = f32[2048,4096]{1,0:T(8,128)} fusion(bf16[2048,224]{0,1:T(8,128)(2,1)S(1)} %get-tuple-element.9, bf16[224,4096]{1,0:T(8,128)(2,1)} %get-tuple-element.43), kind=kOutput, calls=%fused_computation.133 | convolution fusion | flops 3758096384 | bytes 36306944 | tf_op jit(solution)/shard_map/dot_general | solution.py:48
  219.6 16.9 %add_convert_fusion = bf16[2048,4096]{1,0:T(8,128)(2,1)} fusion(f32[2048,4096]{1,0:T(8,128)} %fusion.38, bf16[2048,224]{0,1:T(8,128)(2,1)S(1)} %get-tuple-element.8, bf16[224,4096]{1,0:T(8,128)(2,1)S(1)} %get-tuple-element.11), kind=kOutput, calls=%fused_computation | convolution fusion | flops 3774873600 | bytes 53084160 | tf_op jit(solution)/shard_map/dot_general | solution.py:49
  236.6 26.3 %reduce-scatter.3.cloned.1.call-done = bf16[2048,2048]{1,0:T(8,128)(2,1)} async-done(((bf16[2048,4096]{1,0:T(8,128)(2,1)}), bf16[2048,2048]{1,0:T(8,128)(2,1)}) %reduce-scatter.3.cloned.1.call-update) | async-done | bytes 8388624 | tf_op jit(solution)/shard_map/reduce_scatter | solution.py:50
  265.1 6.9 %all-to-all-start = ((bf16[16,128,224]{1,2,0:T(8,128)(2,1)}), bf16[16,128,224]{1,2,0:T(8,128)(2,1)S(1)}, u32[]{:S(2)}, u32[]{:S(2)}) async-start(bf16[16,128,224]{1,2,0:T(8,128)(2,1)} %bitcast.73), calls=%async_computation | async-start | bytes 1835008 | tf_op jit(solution)/shard_map/all_to_all | solution.py:47
  272.1 5.9 %fusion.6 = f32[224,2048]{1,0:T(8,128)S(1)} fusion(bf16[2048,224]{0,1:T(8,128)(2,1)S(1)} %copy-done.4, bf16[4096,2048]{1,0:T(8,128)(2,1)} %all-gather.6.cloned.1.call-done), kind=kOutput, calls=%fused_computation.7 | convolution fusion | flops 1879048192 | bytes 11141120 | tf_op jit(solution)/shard_map/dot_general | solution.py:57
  278.0 5.6 %fusion.14 = f32[224,2048]{1,0:T(8,128)S(1)} fusion(bf16[2048,224]{0,1:T(8,128)(2,1)S(1)} %copy-done.4, bf16[4096,2048]{1,0:T(8,128)(2,1)} %all-gather.6.cloned.1.call-done), kind=kOutput, calls=%fused_computation.15 | convolution fusion | flops 1879048192 | bytes 11141120 | tf_op jit(solution)/shard_map/dot_general | solution.py:57
  283.8 2.1 fusion
  285.9 2.1 fusion.8
  288.1 3.5 maximum_multiply_fusion
  291.6 14.6 %all-to-all-done = bf16[16,128,224]{1,2,0:T(8,128)(2,1)S(1)} async-done(((bf16[16,128,224]{1,2,0:T(8,128)(2,1)}), bf16[16,128,224]{1,2,0:T(8,128)(2,1)S(1)}, u32[]{:S(2)}, u32[]{:S(2)}) %all-to-all-start) | async-done | bytes 917536 | tf_op jit(solution)/shard_map/all_to_all | solution.py:47
  307.5 151.2 %reduce-scatter.5.cloned.1.call-done = bf16[128,2048]{1,0:T(8,128)(2,1)} async-done(((bf16[2048,2048]{1,0:T(8,128)(2,1)}), bf16[128,2048]{1,0:T(8,128)(2,1)}) %reduce-scatter.5.cloned.1.call-update) | async-done | bytes 524304 | tf_op jit(solution)/shard_map/reduce_scatter | solution.py:53
  (73 shorter events, 41.2 us)
Async XLA Ops:
  7.2 114.8 %all-gather.4.cloned.1.call-start = ((), (), s32[]{:S(2)}) async-start(), calls=%async_computation.4 | async-start | bytes 8912896 | tf_op jit(solution)/shard_map/all_gather | solution.py:20
  7.9 168.2 %all-gather.6.cloned.1.call-start = ((), (), s32[]{:S(2)}) async-start(), calls=%async_computation.7 | async-start | bytes 25165824 | tf_op jit(solution)/shard_map/all_gather | solution.py:21
  122.0 1.2 copy-start
  123.1 7.6 %copy-start.5 = (f32[224,16]{0,1:T(8,128)S(1)}, f32[224,16]{0,1:T(8,128)}, u32[]{:S(2)}) copy-start(f32[224,16]{0,1:T(8,128)} %param.8) | copy-start | bytes 43012
  123.1 7.6 %copy-start.6 = (f32[224,16]{0,1:T(8,128)S(1)}, f32[224,16]{0,1:T(8,128)}, u32[]{:S(2)}) copy-start(f32[224,16]{0,1:T(8,128)} %param.10) | copy-start | bytes 43012
  124.4 70.0 %all-to-all-start.1 = ((bf16[128,16,224]{0,2,1:T(8,128)(2,1)}), bf16[128,16,224]{0,2,1:T(8,128)(2,1)S(1)}, u32[]{:S(2)}, u32[]{:S(2)}) async-start(bf16[128,16,224]{0,2,1:T(8,128)(2,1)} %bitcast.36), calls=%async_computation.1 | async-start | bytes 1835008 | tf_op jit(solution)/shard_map/all_to_all | solution.py:23
  130.7 132.2 %reduce-scatter.3.cloned.1.call-start = ((), (), s32[]{:S(2)}) async-start(), calls=%async_computation.5 | async-start | bytes 25165824 | tf_op jit(solution)/shard_map/reduce_scatter | solution.py:50
  139.2 1.0 copy-start.8
  154.6 14.8 %copy-start.9 = (bf16[224,2048]{1,0:T(8,128)(2,1)}, bf16[224,2048]{1,0:T(8,128)(2,1)S(1)}, u32[]{:S(2)}) copy-start(bf16[224,2048]{1,0:T(8,128)(2,1)S(1)} %get-tuple-element.60) | copy-start | bytes 2752516
  163.4 0.9 copy-start.7
  176.1 14.4 %copy-start.11 = (bf16[4096,2048]{1,0:T(8,128)(2,1)S(1)}, bf16[4096,2048]{1,0:T(8,128)(2,1)}, u32[]{:S(2)}) copy-start(bf16[4096,2048]{1,0:T(8,128)(2,1)} %all-gather.6.cloned.1.call-done) | copy-start | bytes 50331652
  183.8 6.7 %copy-start.10 = (bf16[224,2048]{1,0:T(8,128)(2,1)S(1)}, bf16[224,2048]{1,0:T(8,128)(2,1)}, u32[]{:S(2)}) copy-start(bf16[224,2048]{1,0:T(8,128)(2,1)} %copy-done.9) | copy-start | bytes 2752516
  194.4 0.9 copy-start.1
  204.6 15.0 %copy-start.3 = (bf16[2048,224]{0,1:T(8,128)(2,1)}, bf16[2048,224]{0,1:T(8,128)(2,1)S(1)}, u32[]{:S(2)}) copy-start(bf16[2048,224]{0,1:T(8,128)(2,1)S(1)} %get-tuple-element.8) | copy-start | bytes 2752516
  236.5 222.2 %reduce-scatter.5.cloned.1.call-start = ((), (), s32[]{:S(2)}) async-start(), calls=%async_computation.6 | async-start | bytes 8912896 | tf_op jit(solution)/shard_map/reduce_scatter | solution.py:53
  262.9 1.2 copy-start.2
  264.0 8.0 %copy-start.4 = (bf16[2048,224]{0,1:T(8,128)(2,1)S(1)}, bf16[2048,224]{0,1:T(8,128)(2,1)}, u32[]{:S(2)}) copy-start(bf16[2048,224]{0,1:T(8,128)(2,1)} %copy-done.3) | copy-start | bytes 2752516
  265.1 41.1 %all-to-all-start = ((bf16[16,128,224]{1,2,0:T(8,128)(2,1)}), bf16[16,128,224]{1,2,0:T(8,128)(2,1)S(1)}, u32[]{:S(2)}, u32[]{:S(2)}) async-start(bf16[16,128,224]{1,2,0:T(8,128)(2,1)} %bitcast.73), calls=%async_computation | async-start | bytes 1835008 | tf_op jit(solution)/shard_map/all_to_all | solution.py:47
  272.1 11.5 %slice-start = ((s8[16777216]{0:T(1024)(128)(4,1)}), s8[4194304]{0:T(1024)(128)(4,1)S(1)}, s32[]{:S(2)}) async-start(s8[16777216]{0:T(1024)(128)(4,1)} %bitcast.107), calls=%async_computation.8 | async-start | bytes 8388608
  272.1 11.5 %slice-start.1 = ((s8[16777216]{0:T(1024)(128)(4,1)}), s8[4194304]{0:T(1024)(128)(4,1)S(1)}, s32[]{:S(2)}) async-start(s8[16777216]{0:T(1024)(128)(4,1)} %bitcast.107), calls=%async_computation.9 | async-start | bytes 8388608
  277.9 5.6 %slice-start.2 = ((s8[16777216]{0:T(1024)(128)(4,1)}), s8[4194304]{0:T(1024)(128)(4,1)S(1)}, s32[]{:S(2)}) async-start(s8[16777216]{0:T(1024)(128)(4,1)} %bitcast.107), calls=%async_computation.10 | async-start | bytes 8388608
  278.0 5.8 %slice-start.3 = ((s8[16777216]{0:T(1024)(128)(4,1)}), s8[4194304]{0:T(1024)(128)(4,1)S(1)}, s32[]{:S(2)}) async-start(s8[16777216]{0:T(1024)(128)(4,1)} %bitcast.107), calls=%async_computation.11 | async-start | bytes 8388608
Sparse Core Ops, SparseCore 0:
  10.7 111.1 all-gather.3
  123.5 30.5 all-gather.5
  236.6 26.1 reduce-scatter.2
  265.6 193.1 reduce-scatter.4
where the time goes:
time: 467 us; the launch traced here: 465 us
  waiting for transfers between devices  307 us (66%)
  matrix products  75.2 us (16%)
  other arithmetic  46.8 us (10%)
  between operations  14.1 us (3%)
  starting transfers between devices  13.3 us (3%)
  local copies, waits for them, and re-layouts  8.98 us (2%)
    reduce_scatter x1, waiting for transfers between devices, per_device(): lax.psum_scatter(partial_sum, 'inter', scatter_dimension=0, tiled=True)  151 us
    all_gather x1, waiting for transfers between devices, per_device(): mine = lax.all_gather(tokens, 'inter', axis=0, tiled=True)  114 us
    unnamed x31, other arithmetic  40.6 us
    dot_general x4, matrix products, forward(): lax.dot_general(whole[s], weights[:, s * wide:(s + 1) * wide], (((1,), (1...  27.5 us
    reduce_scatter x1, waiting for transfers between devices, per_device(): lax.psum_scatter(partial_sum.astype(jnp.bfloat16), 'intra', scatter_dimen...  26.3 us
    dot_general x1, matrix products, per_device(): jnp.dot(d_up, w_up, preferred_element_type=jnp.float32)  16.9 us
    dot_general x4, matrix products, rows_grad(): lax.dot_general(d_rows, whole[s], (((0,), (0,)), ((), ())), preferred_ele...  15.7 us
    dot_general x1, matrix products, per_device(): partial_sum = jnp.dot(d_gate, w_gate, preferred_element_type=jnp.float32)  15 us
  transfers between devices with their start and end apart: 6, of which 4 were waited for; matrix products, arithmetic and copies ran while one was open for 18% of the time, Pallas kernels for 0%

commit v1 on v0

--- a/solution.py
+++ b/solution.py
@@ -17,7 +17,16 @@
 
 def per_device(tokens, gate_codes, gate_scales, up_codes, up_scales, cotangent):
     groups = lax.axis_size("inter")
-    mine = lax.all_gather(tokens, "inter", axis=0, tiled=True)
+    array = tokens
+    ways, here, hop = (lax.axis_size("inter"), lax.axis_index("inter"), array.shape[0])
+    lengths = [n * ways if d == 0 else n for d, n in enumerate(array.shape)]
+    full = lax.dynamic_update_slice_in_dim(
+        jnp.zeros(lengths, array.dtype), array, here * hop, axis=0
+    )
+    for far in range(1, ways):
+        array = lax.ppermute(array, "inter", [(d, (d + 1) % ways) for d in range(ways)])
+        full = lax.dynamic_update_slice_in_dim(full, array, (here - far) % ways * hop, axis=0)
+    mine = full
     whole = lax.all_gather(mine, "intra", axis=0, tiled=False)
     slabs, count, wide = whole.shape
     back = lax.all_to_all(cotangent, "inter", split_axis=1, concat_axis=0, tiled=True)

time: 467 us -> 583 us (1.25)
  starting transfers between devices: 13.3 us -> 92.4 us
  waiting for transfers between devices: 307 us -> 327 us
  local copies, waits for them, and re-layouts: 8.98 us -> 28.9 us
    ppermute x0 -> x15, waiting for transfers between devices: none -> 136 us  [per_device(): lax.ppermute(array, 'inter', [(d, (d + 1) % ways) for d in range(ways)])]
    all_gather x1 -> x0, waiting for transfers between devices: 114 us -> none  [per_device(): mine = lax.all_gather(tokens, 'inter', axis=0, tiled=True)]
    ppermute x0 -> x15, starting transfers between devices: none -> 64.4 us  [per_device(): lax.ppermute(array, 'inter', [(d, (d + 1) % ways) for d in range(ways)])]
    all_to_all x1, starting transfers between devices: 6.25 us -> 20.8 us  [per_device(): lax.all_to_all(cotangent, 'inter', split_axis=1, concat_axis=0, tiled=True)]
    dynamic_update_slice x0 -> x16, local copies, waits for them, and re-layouts: none -> 13.5 us  [the longest x15 12.6 us: per_device(): lax.dynamic_update_slice_in_dim(full, array, (here - far) % ways * hop, a...]
  transfers between devices with their start and end apart: 6 -> 20, of which waited for: 4 -> 18; matrix products, arithmetic and copies ran while one was open for 18% -> 16% of each run, Pallas kernels for 0% -> 0%
where the time goes in v1:
time: 583 us; the launch traced here: 581 us
  waiting for transfers between devices  327 us (56%)
  starting transfers between devices  92.4 us (16%)
  matrix products  72.6 us (12%)
  other arithmetic  46.7 us (8%)
  local copies, waits for them, and re-layouts  28.9 us (5%)
  between operations  14.1 us (2%)
    reduce_scatter x1, waiting for transfers between devices, per_device(): lax.psum_scatter(partial_sum, 'inter', scatter_dimension=0, tiled=True)  149 us
    ppermute x15, waiting for transfers between devices, per_device(): lax.ppermute(array, 'inter', [(d, (d + 1) % ways) for d in range(ways)])  136 us
    ppermute x15, starting transfers between devices, per_device(): lax.ppermute(array, 'inter', [(d, (d + 1) % ways) for d in range(ways)])  64.4 us
    unnamed x31, other arithmetic  40.4 us
    reduce_scatter x1, waiting for transfers between devices, per_device(): lax.psum_scatter(partial_sum.astype(jnp.bfloat16), 'intra', scatter_dimen...  26.3 us
    dot_general x4, matrix products, forward(): lax.dot_general(whole[s], weights[:, s * wide:(s + 1) * wide], (((1,), (1...  24.9 us
    all_to_all x1, starting transfers between devices, per_device(): lax.all_to_all(cotangent, 'inter', split_axis=1, concat_axis=0, tiled=True)  20.8 us
    dot_general x1, matrix products, per_device(): jnp.dot(d_up, w_up, preferred_element_type=jnp.float32)  16.9 us
  transfers between devices with their start and end apart: 20, of which 18 were waited for; matrix products, arithmetic and copies ran while one was open for 16% of the time, Pallas kernels for 0%

profile of v1, /device:TPU:26, one launch (start us, length us, event | category | flops | bytes accessed | tf_op | source)
XLA Modules:
  0.0 581.4 jit_solution(12604652621069001256)
XLA Ops:
  8.8 12.4 %collective-permute-done = bf16[128,2048]{1,0:T(8,128)(2,1)S(1)} collective-permute-done((bf16[128,2048]{1,0:T(8,128)(2,1)}, bf16[128,2048]{1,0:T(8,128)(2,1)S(1)}, u32[]{:S(2)}, u32[]{:S(2)}) %collective-permute-start) | collective-permute-done | bytes 524320 | tf_op jit(solution)/shard_map/ppermute | solution.py:27
  23.5 11.0 %collective-permute-done.1 = bf16[128,2048]{1,0:T(8,128)(2,1)S(1)} collective-permute-done((bf16[128,2048]{1,0:T(8,128)(2,1)S(1)}, bf16[128,2048]{1,0:T(8,128)(2,1)S(1)}, u32[]{:S(2)}, u32[]{:S(2)}) %collective-permute-start.1) | collective-permute-done | bytes 524320 | tf_op jit(solution)/shard_map/ppermute | solution.py:27
  37.2 11.0 %collective-permute-done.2 = bf16[128,2048]{1,0:T(8,128)(2,1)S(1)} collective-permute-done((bf16[128,2048]{1,0:T(8,128)(2,1)S(1)}, bf16[128,2048]{1,0:T(8,128)(2,1)S(1)}, u32[]{:S(2)}, u32[]{:S(2)}) %collective-permute-start.2) | collective-permute-done | bytes 524320 | tf_op jit(solution)/shard_map/ppermute | solution.py:27
  50.1 11.1 %collective-permute-done.3 = bf16[128,2048]{1,0:T(8,128)(2,1)S(1)} collective-permute-done((bf16[128,2048]{1,0:T(8,128)(2,1)S(1)}, bf16[128,2048]{1,0:T(8,128)(2,1)S(1)}, u32[]{:S(2)}, u32[]{:S(2)}) %collective-permute-start.3) | collective-permute-done | bytes 524320 | tf_op jit(solution)/shard_map/ppermute | solution.py:27
  63.3 9.9 %collective-permute-done.4 = bf16[128,2048]{1,0:T(8,128)(2,1)S(1)} collective-permute-done((bf16[128,2048]{1,0:T(8,128)(2,1)S(1)}, bf16[128,2048]{1,0:T(8,128)(2,1)S(1)}, u32[]{:S(2)}, u32[]{:S(2)}) %collective-permute-start.4) | collective-permute-done | bytes 524320 | tf_op jit(solution)/shard_map/ppermute | solution.py:27
  77.5 7.9 %collective-permute-done.5 = bf16[128,2048]{1,0:T(8,128)(2,1)S(1)} collective-permute-done((bf16[128,2048]{1,0:T(8,128)(2,1)S(1)}, bf16[128,2048]{1,0:T(8,128)(2,1)S(1)}, u32[]{:S(2)}, u32[]{:S(2)}) %collective-permute-start.5) | collective-permute-done | bytes 524320 | tf_op jit(solution)/shard_map/ppermute | solution.py:27
  90.7 7.1 %collective-permute-done.6 = bf16[128,2048]{1,0:T(8,128)(2,1)S(1)} collective-permute-done((bf16[128,2048]{1,0:T(8,128)(2,1)S(1)}, bf16[128,2048]{1,0:T(8,128)(2,1)S(1)}, u32[]{:S(2)}, u32[]{:S(2)}) %collective-permute-start.6) | collective-permute-done | bytes 524320 | tf_op jit(solution)/shard_map/ppermute | solution.py:27
  118.8 8.6 %collective-permute-done.8 = bf16[128,2048]{1,0:T(8,128)(2,1)S(1)} collective-permute-done((bf16[128,2048]{1,0:T(8,128)(2,1)S(1)}, bf16[128,2048]{1,0:T(8,128)(2,1)S(1)}, u32[]{:S(2)}, u32[]{:S(2)}) %collective-permute-start.8) | collective-permute-done | bytes 524320 | tf_op jit(solution)/shard_map/ppermute | solution.py:27
  133.8 10.0 %collective-permute-done.9 = bf16[128,2048]{1,0:T(8,128)(2,1)S(1)} collective-permute-done((bf16[128,2048]{1,0:T(8,128)(2,1)S(1)}, bf16[128,2048]{1,0:T(8,128)(2,1)S(1)}, u32[]{:S(2)}, u32[]{:S(2)}) %collective-permute-start.9) | collective-permute-done | bytes 524320 | tf_op jit(solution)/shard_map/ppermute | solution.py:27
  150.0 10.1 %collective-permute-done.10 = bf16[128,2048]{1,0:T(8,128)(2,1)S(1)} collective-permute-done((bf16[128,2048]{1,0:T(8,128)(2,1)S(1)}, bf16[128,2048]{1,0:T(8,128)(2,1)S(1)}, u32[]{:S(2)}, u32[]{:S(2)}) %collective-permute-start.10) | collective-permute-done | bytes 524320 | tf_op jit(solution)/shard_map/ppermute | solution.py:27
  167.3 10.2 %collective-permute-done.11 = bf16[128,2048]{1,0:T(8,128)(2,1)S(1)} collective-permute-done((bf16[128,2048]{1,0:T(8,128)(2,1)S(1)}, bf16[128,2048]{1,0:T(8,128)(2,1)S(1)}, u32[]{:S(2)}, u32[]{:S(2)}) %collective-permute-start.11) | collective-permute-done | bytes 524320 | tf_op jit(solution)/shard_map/ppermute | solution.py:27
  177.5 6.7 %collective-permute-start.12 = (bf16[128,2048]{1,0:T(8,128)(2,1)S(1)}, bf16[128,2048]{1,0:T(8,128)(2,1)S(1)}, u32[]{:S(2)}, u32[]{:S(2)}) collective-permute-start(bf16[128,2048]{1,0:T(8,128)(2,1)S(1)} %collective-permute-done.11), channel_id=1, source_target_pairs={{0,2},{2,4},{4,6},{6,8},{8,10},{10,12},{12,14},{14,16},{16,18},{18... | collective-permute-start | bytes 1572872 | tf_op jit(solution)/shard_map/ppermute | solution.py:27
  185.8 10.0 %collective-permute-done.12 = bf16[128,2048]{1,0:T(8,128)(2,1)S(1)} collective-permute-done((bf16[128,2048]{1,0:T(8,128)(2,1)S(1)}, bf16[128,2048]{1,0:T(8,128)(2,1)S(1)}, u32[]{:S(2)}, u32[]{:S(2)}) %collective-permute-start.12) | collective-permute-done | bytes 524320 | tf_op jit(solution)/shard_map/ppermute | solution.py:27
  203.4 8.8 %collective-permute-done.13 = bf16[128,2048]{1,0:T(8,128)(2,1)S(1)} collective-permute-done((bf16[128,2048]{1,0:T(8,128)(2,1)S(1)}, bf16[128,2048]{1,0:T(8,128)(2,1)S(1)}, u32[]{:S(2)}, u32[]{:S(2)}) %collective-permute-start.13) | collective-permute-done | bytes 524320 | tf_op jit(solution)/shard_map/ppermute | solution.py:27
  212.2 6.1 %collective-permute-start.14 = (bf16[128,2048]{1,0:T(8,128)(2,1)S(1)}, bf16[128,2048]{1,0:T(8,128)(2,1)S(1)}, u32[]{:S(2)}, u32[]{:S(2)}) collective-permute-start(bf16[128,2048]{1,0:T(8,128)(2,1)S(1)} %collective-permute-done.13), channel_id=1, source_target_pairs={{0,2},{2,4},{4,6},{6,8},{8,10},{10,12},{12,14},{14,16},{16,18},{18... | collective-permute-start | bytes 1572872 | tf_op jit(solution)/shard_map/ppermute | solution.py:27
  228.3 20.8 %all-to-all-start.1 = ((bf16[128,16,224]{0,2,1:T(8,128)(2,1)}), bf16[128,16,224]{0,2,1:T(8,128)(2,1)S(1)}, u32[]{:S(2)}, u32[]{:S(2)}) async-start(bf16[128,16,224]{0,2,1:T(8,128)(2,1)} %bitcast.52), calls=%async_computation.1 | async-start | bytes 1835008 | tf_op jit(solution)/shard_map/all_to_all | solution.py:32
  294.5 6.4 %fusion.6 = f32[2048,224]{0,1:T(8,128)S(1)} fusion(bf16[224,2048]{1,0:T(8,128)(2,1)} %copy-done.12, bf16[2,2048,2048]{2,1,0:T(8,128)(2,1)} %all-gather.2.cloned.1.call-done), kind=kOutput, calls=%fused_computation.9 | convolution fusion | flops 1879048192 | bytes 11141120 | tf_op jit(solution)/shard_map/dot_general | solution.py:39
  312.9 9.5 %fusion.13 = (bf16[2048,224]{0,1:T(8,128)(2,1)S(1)}, bf16[2048,224]{0,1:T(8,128)(2,1)S(1)}, bf16[28,16,8,128]{3,2,1,0:T(8,128)(2,1)}) fusion(f32[2048,224]{0,1:T(8,128)} %fusion.9, f32[2048,224]{0,1:T(8,128)} %fusion.7, bf16[224,2048]{1,0:T(8,128)(2,1)} %copy-done.15, bf16[2,2048,2048]{2,1,0:T(8,128)(2,1)} %all-gather.2.cloned.1.call-done, ...), kind=kOutput, calls=%fused_computation.20 | convolution fusion | flops 1886846976 | bytes 16646144 | tf_op jit(solution)/shard_map/dot_general | solution.py:39
  322.4 15.0 %fusion.18 = f32[2048,4096]{1,0:T(8,128)} fusion(bf16[2048,224]{0,1:T(8,128)(2,1)S(1)} %get-tuple-element.13, bf16[224,4096]{1,0:T(8,128)(2,1)} %get-tuple-element.47), kind=kOutput, calls=%fused_computation.141 | convolution fusion | flops 3758096384 | bytes 36306944 | tf_op jit(solution)/shard_map/dot_general | solution.py:57
  337.4 16.9 %add_convert_fusion = bf16[2048,4096]{1,0:T(8,128)(2,1)} fusion(f32[2048,4096]{1,0:T(8,128)} %fusion.18, bf16[2048,224]{0,1:T(8,128)(2,1)S(1)} %get-tuple-element.12, bf16[224,4096]{1,0:T(8,128)(2,1)S(1)} %get-tuple-element.15), kind=kOutput, calls=%fused_computation | convolution fusion | flops 3774873600 | bytes 53084160 | tf_op jit(solution)/shard_map/dot_general | solution.py:58
  354.5 26.3 %reduce-scatter.3.cloned.1.call-done = bf16[2048,2048]{1,0:T(8,128)(2,1)} async-done(((bf16[2048,4096]{1,0:T(8,128)(2,1)}), bf16[2048,2048]{1,0:T(8,128)(2,1)}) %reduce-scatter.3.cloned.1.call-update) | async-done | bytes 8388624 | tf_op jit(solution)/shard_map/reduce_scatter | solution.py:59
  383.0 6.9 %all-to-all-start = ((bf16[16,128,224]{1,2,0:T(8,128)(2,1)}), bf16[16,128,224]{1,2,0:T(8,128)(2,1)S(1)}, u32[]{:S(2)}, u32[]{:S(2)}) async-start(bf16[16,128,224]{1,2,0:T(8,128)(2,1)} %bitcast.117), calls=%async_computation | async-start | bytes 1835008 | tf_op jit(solution)/shard_map/all_to_all | solution.py:56
  409.6 14.6 %all-to-all-done = bf16[16,128,224]{1,2,0:T(8,128)(2,1)S(1)} async-done(((bf16[16,128,224]{1,2,0:T(8,128)(2,1)}), bf16[16,128,224]{1,2,0:T(8,128)(2,1)S(1)}, u32[]{:S(2)}, u32[]{:S(2)}) %all-to-all-start) | async-done | bytes 917536 | tf_op jit(solution)/shard_map/all_to_all | solution.py:56
  425.5 149.4 %reduce-scatter.5.cloned.1.call-done = bf16[128,2048]{1,0:T(8,128)(2,1)} async-done(((bf16[2048,2048]{1,0:T(8,128)(2,1)}), bf16[128,2048]{1,0:T(8,128)(2,1)}) %reduce-scatter.5.cloned.1.call-update) | async-done | bytes 524304 | tf_op jit(solution)/shard_map/reduce_scatter | solution.py:62
  (127 shorter events, 160.6 us)
Async XLA Ops:
  7.2 287.4 %all-gather.2.cloned.1.call-start = ((), (), s32[]{:S(2)}) async-start(), calls=%async_computation.4 | async-start | bytes 25165824 | tf_op jit(solution)/shard_map/all_gather | solution.py:30
  7.2 13.9 %collective-permute-start = (bf16[128,2048]{1,0:T(8,128)(2,1)}, bf16[128,2048]{1,0:T(8,128)(2,1)S(1)}, u32[]{:S(2)}, u32[]{:S(2)}) collective-permute-start(bf16[128,2048]{1,0:T(8,128)(2,1)} %param.6), channel_id=1, source_target_pairs={{0,2},{2,4},{4,6},{6,8},{8,10},{10,12},{12,14},{14,16},{16,18},{18... | collective-permute-start | bytes 1572872 | tf_op jit(solution)/shard_map/ppermute | solution.py:27
  21.1 13.4 %collective-permute-start.1 = (bf16[128,2048]{1,0:T(8,128)(2,1)S(1)}, bf16[128,2048]{1,0:T(8,128)(2,1)S(1)}, u32[]{:S(2)}, u32[]{:S(2)}) collective-permute-start(bf16[128,2048]{1,0:T(8,128)(2,1)S(1)} %collective-permute-done), channel_id=1, source_target_pairs={{0,2},{2,4},{4,6},{6,8},{8,10},{10,12},{12,14},{14,16},{16,18},{18... | collective-permute-start | bytes 1572872 | tf_op jit(solution)/shard_map/ppermute | solution.py:27
  34.5 13.8 %collective-permute-start.2 = (bf16[128,2048]{1,0:T(8,128)(2,1)S(1)}, bf16[128,2048]{1,0:T(8,128)(2,1)S(1)}, u32[]{:S(2)}, u32[]{:S(2)}) collective-permute-start(bf16[128,2048]{1,0:T(8,128)(2,1)S(1)} %collective-permute-done.1), channel_id=1, source_target_pairs={{0,2},{2,4},{4,6},{6,8},{8,10},{10,12},{12,14},{14,16},{16,18},{18... | collective-permute-start | bytes 1572872 | tf_op jit(solution)/shard_map/ppermute | solution.py:27
  48.3 12.9 %collective-permute-start.3 = (bf16[128,2048]{1,0:T(8,128)(2,1)S(1)}, bf16[128,2048]{1,0:T(8,128)(2,1)S(1)}, u32[]{:S(2)}, u32[]{:S(2)}) collective-permute-start(bf16[128,2048]{1,0:T(8,128)(2,1)S(1)} %collective-permute-done.2), channel_id=1, source_target_pairs={{0,2},{2,4},{4,6},{6,8},{8,10},{10,12},{12,14},{14,16},{16,18},{18... | collective-permute-start | bytes 1572872 | tf_op jit(solution)/shard_map/ppermute | solution.py:27
  61.2 36.6 %copy-start.6 = (bf16[128,2048]{1,0:T(8,128)(2,1)}, bf16[128,2048]{1,0:T(8,128)(2,1)S(1)}, u32[]{:S(2)}) copy-start(bf16[128,2048]{1,0:T(8,128)(2,1)S(1)} %collective-permute-done.3) | copy-start | bytes 1572868
  61.2 12.1 %collective-permute-start.4 = (bf16[128,2048]{1,0:T(8,128)(2,1)S(1)}, bf16[128,2048]{1,0:T(8,128)(2,1)S(1)}, u32[]{:S(2)}, u32[]{:S(2)}) collective-permute-start(bf16[128,2048]{1,0:T(8,128)(2,1)S(1)} %collective-permute-done.3), channel_id=1, source_target_pairs={{0,2},{2,4},{4,6},{6,8},{8,10},{10,12},{12,14},{14,16},{16,18},{18... | collective-permute-start | bytes 1572872 | tf_op jit(solution)/shard_map/ppermute | solution.py:27
  73.3 12.1 %collective-permute-start.5 = (bf16[128,2048]{1,0:T(8,128)(2,1)S(1)}, bf16[128,2048]{1,0:T(8,128)(2,1)S(1)}, u32[]{:S(2)}, u32[]{:S(2)}) collective-permute-start(bf16[128,2048]{1,0:T(8,128)(2,1)S(1)} %collective-permute-done.4), channel_id=1, source_target_pairs={{0,2},{2,4},{4,6},{6,8},{8,10},{10,12},{12,14},{14,16},{16,18},{18... | collective-permute-start | bytes 1572872 | tf_op jit(solution)/shard_map/ppermute | solution.py:27
  85.4 12.5 %collective-permute-start.6 = (bf16[128,2048]{1,0:T(8,128)(2,1)S(1)}, bf16[128,2048]{1,0:T(8,128)(2,1)S(1)}, u32[]{:S(2)}, u32[]{:S(2)}) collective-permute-start(bf16[128,2048]{1,0:T(8,128)(2,1)S(1)} %collective-permute-done.5), channel_id=1, source_target_pairs={{0,2},{2,4},{4,6},{6,8},{8,10},{10,12},{12,14},{14,16},{16,18},{18... | collective-permute-start | bytes 1572872 | tf_op jit(solution)/shard_map/ppermute | solution.py:27
  97.8 14.2 %collective-permute-start.7 = (bf16[128,2048]{1,0:T(8,128)(2,1)S(1)}, bf16[128,2048]{1,0:T(8,128)(2,1)S(1)}, u32[]{:S(2)}, u32[]{:S(2)}) collective-permute-start(bf16[128,2048]{1,0:T(8,128)(2,1)S(1)} %collective-permute-done.6), channel_id=1, source_target_pairs={{0,2},{2,4},{4,6},{6,8},{8,10},{10,12},{12,14},{14,16},{16,18},{18... | collective-permute-start | bytes 1572872 | tf_op jit(solution)/shard_map/ppermute | solution.py:27
  108.8 24.2 %copy-start.7 = (bf16[128,2048]{1,0:T(8,128)(2,1)S(1)}, bf16[128,2048]{1,0:T(8,128)(2,1)}, u32[]{:S(2)}) copy-start(bf16[128,2048]{1,0:T(8,128)(2,1)} %copy-done.6) | copy-start | bytes 1572868
  112.0 15.3 %collective-permute-start.8 = (bf16[128,2048]{1,0:T(8,128)(2,1)S(1)}, bf16[128,2048]{1,0:T(8,128)(2,1)S(1)}, u32[]{:S(2)}, u32[]{:S(2)}) collective-permute-start(bf16[128,2048]{1,0:T(8,128)(2,1)S(1)} %collective-permute-done.7), channel_id=1, source_target_pairs={{0,2},{2,4},{4,6},{6,8},{8,10},{10,12},{12,14},{14,16},{16,18},{18... | collective-permute-start | bytes 1572872 | tf_op jit(solution)/shard_map/ppermute | solution.py:27
  127.3 16.5 %collective-permute-start.9 = (bf16[128,2048]{1,0:T(8,128)(2,1)S(1)}, bf16[128,2048]{1,0:T(8,128)(2,1)S(1)}, u32[]{:S(2)}, u32[]{:S(2)}) collective-permute-start(bf16[128,2048]{1,0:T(8,128)(2,1)S(1)} %collective-permute-done.8), channel_id=1, source_target_pairs={{0,2},{2,4},{4,6},{6,8},{8,10},{10,12},{12,14},{14,16},{16,18},{18... | collective-permute-start | bytes 1572872 | tf_op jit(solution)/shard_map/ppermute | solution.py:27
  143.8 16.3 %collective-permute-start.10 = (bf16[128,2048]{1,0:T(8,128)(2,1)S(1)}, bf16[128,2048]{1,0:T(8,128)(2,1)S(1)}, u32[]{:S(2)}, u32[]{:S(2)}) collective-permute-start(bf16[128,2048]{1,0:T(8,128)(2,1)S(1)} %collective-permute-done.9), channel_id=1, source_target_pairs={{0,2},{2,4},{4,6},{6,8},{8,10},{10,12},{12,14},{14,16},{16,18},{18... | collective-permute-start | bytes 1572872 | tf_op jit(solution)/shard_map/ppermute | solution.py:27
  160.1 17.4 %collective-permute-start.11 = (bf16[128,2048]{1,0:T(8,128)(2,1)S(1)}, bf16[128,2048]{1,0:T(8,128)(2,1)S(1)}, u32[]{:S(2)}, u32[]{:S(2)}) collective-permute-start(bf16[128,2048]{1,0:T(8,128)(2,1)S(1)} %collective-permute-done.10), channel_id=1, source_target_pairs={{0,2},{2,4},{4,6},{6,8},{8,10},{10,12},{12,14},{14,16},{16,18},{18... | collective-permute-start | bytes 1572872 | tf_op jit(solution)/shard_map/ppermute | solution.py:27
  177.5 18.3 %collective-permute-start.12 = (bf16[128,2048]{1,0:T(8,128)(2,1)S(1)}, bf16[128,2048]{1,0:T(8,128)(2,1)S(1)}, u32[]{:S(2)}, u32[]{:S(2)}) collective-permute-start(bf16[128,2048]{1,0:T(8,128)(2,1)S(1)} %collective-permute-done.11), channel_id=1, source_target_pairs={{0,2},{2,4},{4,6},{6,8},{8,10},{10,12},{12,14},{14,16},{16,18},{18... | collective-permute-start | bytes 1572872 | tf_op jit(solution)/shard_map/ppermute | solution.py:27
  195.8 16.4 %collective-permute-start.13 = (bf16[128,2048]{1,0:T(8,128)(2,1)S(1)}, bf16[128,2048]{1,0:T(8,128)(2,1)S(1)}, u32[]{:S(2)}, u32[]{:S(2)}) collective-permute-start(bf16[128,2048]{1,0:T(8,128)(2,1)S(1)} %collective-permute-done.12), channel_id=1, source_target_pairs={{0,2},{2,4},{4,6},{6,8},{8,10},{10,12},{12,14},{14,16},{16,18},{18... | collective-permute-start | bytes 1572872 | tf_op jit(solution)/shard_map/ppermute | solution.py:27
  212.2 12.8 %collective-permute-start.14 = (bf16[128,2048]{1,0:T(8,128)(2,1)S(1)}, bf16[128,2048]{1,0:T(8,128)(2,1)S(1)}, u32[]{:S(2)}, u32[]{:S(2)}) collective-permute-start(bf16[128,2048]{1,0:T(8,128)(2,1)S(1)} %collective-permute-done.13), channel_id=1, source_target_pairs={{0,2},{2,4},{4,6},{6,8},{8,10},{10,12},{12,14},{14,16},{16,18},{18... | collective-permute-start | bytes 1572872 | tf_op jit(solution)/shard_map/ppermute | solution.py:27
  227.1 22.3 %copy-start.10 = (f32[224,16]{0,1:T(8,128)S(1)}, f32[224,16]{0,1:T(8,128)}, u32[]{:S(2)}) copy-start(f32[224,16]{0,1:T(8,128)} %param.8) | copy-start | bytes 43012
  227.1 22.3 %copy-start.11 = (f32[224,16]{0,1:T(8,128)S(1)}, f32[224,16]{0,1:T(8,128)}, u32[]{:S(2)}) copy-start(f32[224,16]{0,1:T(8,128)} %param.10) | copy-start | bytes 43012
  228.3 83.7 %all-to-all-start.1 = ((bf16[128,16,224]{0,2,1:T(8,128)(2,1)}), bf16[128,16,224]{0,2,1:T(8,128)(2,1)S(1)}, u32[]{:S(2)}, u32[]{:S(2)}) async-start(bf16[128,16,224]{0,2,1:T(8,128)(2,1)} %bitcast.52), calls=%async_computation.1 | async-start | bytes 1835008 | tf_op jit(solution)/shard_map/all_to_all | solution.py:32
  249.1 131.6 %reduce-scatter.3.cloned.1.call-start = ((), (), s32[]{:S(2)}) async-start(), calls=%async_computation.5 | async-start | bytes 25165824 | tf_op jit(solution)/shard_map/reduce_scatter | solution.py:59
  354.4 220.4 %reduce-scatter.5.cloned.1.call-start = ((), (), s32[]{:S(2)}) async-start(), calls=%async_computation.6 | async-start | bytes 8912896 | tf_op jit(solution)/shard_map/reduce_scatter | solution.py:62
  383.0 41.2 %all-to-all-start = ((bf16[16,128,224]{1,2,0:T(8,128)(2,1)}), bf16[16,128,224]{1,2,0:T(8,128)(2,1)S(1)}, u32[]{:S(2)}, u32[]{:S(2)}) async-start(bf16[16,128,224]{1,2,0:T(8,128)(2,1)} %bitcast.117), calls=%async_computation | async-start | bytes 1835008 | tf_op jit(solution)/shard_map/all_to_all | solution.py:56
  (17 other events, 108.3 us)
Sparse Core Ops, SparseCore 0:
  226.0 42.9 all-gather.1
  354.5 26.1 reduce-scatter.2
  383.6 191.1 reduce-scatter.4
